TPU v7x, 512 devices: a whole 4x8x8 slice. The times are simulated.
512 devices in a mesh: gx: 64 (over z_lo, y, core), gy: 8 (over x, z_hi).
Axes of the slice: x: 4, y: 8, z: 8 (z_hi: 2, z_lo: 4; z = z_hi * 4 + z_lo), core: 2. Of those that a mesh axis runs over, the one named last changes fastest.
Arguments:
- velocity: float32 [3, 512, 256, 128], P(None, 'gx', 'gy'), may hold values from -6 to 6
- stress: float32 [6, 512, 256, 128], P(None, 'gx', 'gy'), may hold values from -6 to 6
- lame_lambda: bfloat16 [512, 256, 128], P('gx', 'gy'), may hold values from 0.5 to 1.5
- shear_modulus: bfloat16 [512, 256, 128], P('gx', 'gy'), may hold values from 0.29882812 to 1
- buoyancy: bfloat16 [512, 256, 128], P('gx', 'gy'), may hold values from 0.5 to 1.5
- source_p: bfloat16 [3, 512, 256, 128], P(None, 'gx', 'gy'), may hold values from -6 to 6
- source_s: bfloat16 [3, 512, 256, 128], P(None, 'gx', 'gy'), may hold values from -6 to 6
Outputs:
- image_p: float32 [512, 256, 128], P('gx', 'gy')
- image_s: float32 [512, 256, 128], P('gx', 'gy')
All inputs are finite; a program needn't handle non-finite values.
Results may differ from a plain program's by a relative error of at most 0.0003.
Values sent between devices are 32-bit elements; how exact they have to be, the bound alone decides.
A program may use at most 64 MiB of HBM per device.

v0:
```python
import math
import jax
import jax.numpy as jnp
from jax import lax
from jax.sharding import PartitionSpec as P

STEPS = 2
time_step = 0.2


def passed_along(block, axis, distance):
    devices = range(lax.axis_size(axis))
    route = [(i - distance, i) for i in devices if i - distance in devices]
    return lax.ppermute(block, axis, route)


def x_rims(planes, offset):
    return passed_along(planes, "gx", offset)


def y_rims(planes, offset):
    return passed_along(planes, "gy", offset)


def with_next(field, rim, which):
    length = field.shape[which]
    return jnp.concatenate([lax.slice_in_dim(field, 1, length, axis=which), rim], axis=which)


def with_prior(field, rim, which):
    length = field.shape[which]
    return jnp.concatenate([rim, lax.slice_in_dim(field, 0, length - 1, axis=which)], axis=which)


def zero_rim(field, which):
    return jnp.zeros_like(lax.slice_in_dim(field, 0, 1, axis=which))


def stress_step(velocity, stress, lame_value, shear_value):
    x_speed, y_speed, z_speed = (velocity[0], velocity[1], velocity[2])
    prior_x = x_rims(x_speed[None, -1:], 1)
    next_x = x_rims(jnp.stack([y_speed[:1], z_speed[:1]]), -1)
    prior_y = y_rims(y_speed[None, :, -1:], 1)
    next_y = y_rims(jnp.stack([x_speed[:, :1], z_speed[:, :1]]), -1)
    strain_x = x_speed - with_prior(x_speed, prior_x[0], 0)
    strain_y = y_speed - with_prior(y_speed, prior_y[0], 1)
    strain_z = z_speed - with_prior(z_speed, zero_rim(z_speed, 2), 2)
    volume = strain_x + strain_y + strain_z
    normal_x = stress[0] + time_step * (lame_value * volume + 2.0 * shear_value * strain_x)
    normal_y = stress[1] + time_step * (lame_value * volume + 2.0 * shear_value * strain_y)
    normal_z = stress[2] + time_step * (lame_value * volume + 2.0 * shear_value * strain_z)
    shear_xy = stress[3] + time_step * shear_value * (
        with_next(x_speed, next_y[0], 1) - x_speed + (with_next(y_speed, next_x[0], 0) - y_speed)
    )
    shear_xz = stress[4] + time_step * shear_value * (
        with_next(x_speed, zero_rim(x_speed, 2), 2)
        - x_speed
        + (with_next(z_speed, next_x[1], 0) - z_speed)
    )
    shear_yz = stress[5] + time_step * shear_value * (
        with_next(y_speed, zero_rim(y_speed, 2), 2)
        - y_speed
        + (with_next(z_speed, next_y[1], 1) - z_speed)
    )
    return jnp.stack([normal_x, normal_y, normal_z, shear_xy, shear_xz, shear_yz])


def velocity_step(velocity, stress, buoy_value):
    normal_x, normal_y, normal_z = (stress[0], stress[1], stress[2])
    shear_xy, shear_xz, shear_yz = (stress[3], stress[4], stress[5])
    next_x = x_rims(normal_x[None, :1], -1)
    prior_x = x_rims(jnp.stack([shear_xy[-1:], shear_xz[-1:]]), 1)
    next_y = y_rims(normal_y[None, :, :1], -1)
    prior_y = y_rims(jnp.stack([shear_xy[:, -1:], shear_yz[:, -1:]]), 1)
    x_speed = velocity[0] + time_step * buoy_value * (
        with_next(normal_x, next_x[0], 0)
        - normal_x
        + (shear_xy - with_prior(shear_xy, prior_y[0], 1))
        + (shear_xz - with_prior(shear_xz, zero_rim(shear_xz, 2), 2))
    )
    y_speed = velocity[1] + time_step * buoy_value * (
        shear_xy
        - with_prior(shear_xy, prior_x[0], 0)
        + (with_next(normal_y, next_y[0], 1) - normal_y)
        + (shear_yz - with_prior(shear_yz, zero_rim(shear_yz, 2), 2))
    )
    z_speed = velocity[2] + time_step * buoy_value * (
        shear_xz
        - with_prior(shear_xz, prior_x[1], 0)
        + (shear_yz - with_prior(shear_yz, prior_y[1], 1))
        + (with_next(normal_z, zero_rim(normal_z, 2), 2) - normal_z)
    )
    return jnp.stack([x_speed, y_speed, z_speed])


def phase_tables(length):
    positions = jnp.arange(length, dtype=jnp.int32)
    product = positions[:, None] * positions[None, :] % length
    phases = product.astype(jnp.float32) * (2.0 * math.pi / length)
    return (jnp.cos(phases), jnp.sin(phases))


def z_tables(z_cells, gy_count):
    quarter = z_cells // (2 * gy_count)
    width = gy_count * (quarter + 1)
    column = jnp.arange(width, dtype=jnp.int32)
    block = column // (quarter + 1)
    slot = column % (quarter + 1)
    waves = jnp.where(slot < quarter, block * quarter + slot, z_cells // 2)
    weight = jnp.where(
        slot < quarter, jnp.where(waves == 0, 1.0, 2.0), jnp.where(block == gy_count - 1, 1.0, 0.0)
    ).astype(jnp.float32)
    positions = jnp.arange(z_cells, dtype=jnp.int32)
    product = positions[:, None] * waves[None, :] % z_cells
    phases = product.astype(jnp.float32) * (2.0 * math.pi / z_cells)
    cos_fwd = jnp.cos(phases)
    sin_fwd = jnp.sin(phases)
    cos_back = jnp.transpose(cos_fwd) * weight[:, None]
    sin_back = jnp.transpose(sin_fwd) * weight[:, None]
    return (cos_fwd, sin_fwd, cos_back, sin_back, waves)


def contract(pattern, left, right):
    return jnp.einsum(pattern, left, right, precision=lax.Precision.HIGHEST)


def complex_sum(real_in, imag_in, cosine, sine, pattern, forward_sign):
    cos_real = contract(pattern, real_in, cosine)
    sin_imag = contract(pattern, imag_in, sine)
    cos_imag = contract(pattern, imag_in, cosine)
    sin_real = contract(pattern, real_in, sine)
    if forward_sign:
        return (cos_real + sin_imag, cos_imag - sin_real)
    return (cos_real - sin_imag, cos_imag + sin_real)


def signed_index(positions, length):
    half_length = length // 2
    signed = jnp.where(
        positions < half_length,
        positions,
        jnp.where(positions == half_length, 0, positions - length),
    )
    return signed.astype(jnp.float32)


def forward(velocity, cos_fwd, sin_fwd):
    x_cells, y_cells = (velocity.shape[1], velocity.shape[2])
    gx_count = lax.axis_size("gx")
    gy_count = lax.axis_size("gy")
    x_total = gx_count * x_cells
    y_total = gy_count * y_cells
    kept = cos_fwd.shape[1]
    z_part = kept // gy_count
    y_part = y_total // gx_count
    real_part = contract("cxyn,nk->ckxy", velocity, cos_fwd)
    imag_part = -contract("cxyn,nk->ckxy", velocity, sin_fwd)
    packed = jnp.stack([real_part, imag_part]).reshape(2, 3, 1, kept, x_cells * y_cells)
    arrived = lax.all_to_all(packed, "gy", split_axis=3, concat_axis=2, tiled=True)
    comp_count = arrived.shape[1]
    pieces = arrived.reshape(2, comp_count, gy_count, z_part, x_cells, y_cells)
    cos_y, sin_y = phase_tables(y_total)
    cos_y = cos_y.reshape(gy_count, y_cells, y_total)
    sin_y = sin_y.reshape(gy_count, y_cells, y_total)
    real_out, imag_out = complex_sum(pieces[0], pieces[1], cos_y, sin_y, "cgzxl,glk->ckzx", True)
    after_y = jnp.stack([real_out, imag_out]).reshape(2, comp_count, 1, y_total, z_part * x_cells)
    arrived = lax.all_to_all(after_y, "gx", split_axis=3, concat_axis=2, tiled=True)
    comp_count = arrived.shape[1]
    pieces = arrived.reshape(2, comp_count, gx_count, y_part, z_part, x_cells)
    cos_x, sin_x = phase_tables(x_total)
    cos_x = cos_x.reshape(gx_count, x_cells, x_total)
    sin_x = sin_x.reshape(gx_count, x_cells, x_total)
    real_out, imag_out = complex_sum(pieces[0], pieces[1], cos_x, sin_x, "cgazl,glk->cazk", True)
    return jnp.stack([real_out, imag_out])


def project(spectra, waves, z_total):
    y_part, z_part, x_total = (spectra.shape[2], spectra.shape[3], spectra.shape[4])
    gy_count = lax.axis_size("gy")
    y_total = y_part * lax.axis_size("gx")
    y_index = lax.axis_index("gx") * y_part + jnp.arange(y_part, dtype=jnp.int32)
    z_index = lax.dynamic_slice_in_dim(waves.reshape(gy_count, z_part), lax.axis_index("gy"), 1, 0)[
        0
    ]
    wave_x = signed_index(jnp.arange(x_total, dtype=jnp.int32), x_total)[None, None, :]
    wave_y = signed_index(y_index, y_total)[:, None, None]
    wave_z = signed_index(z_index, z_total)[None, :, None]
    inverse_norm = 1.0 / jnp.maximum(wave_x * wave_x + wave_y * wave_y + wave_z * wave_z, 1.0)
    radial = (
        wave_x * spectra[:, 0] + wave_y * spectra[:, 1] + wave_z * spectra[:, 2]
    ) * inverse_norm
    return jnp.stack([wave_x * radial, wave_y * radial, wave_z * radial], axis=1)


def inverse_fields(spectrum, x_cells, y_cells, z_cells, cos_back, sin_back):
    comp_count, y_part, z_part, x_total = (
        spectrum.shape[1],
        spectrum.shape[2],
        spectrum.shape[3],
        spectrum.shape[4],
    )
    gx_count = lax.axis_size("gx")
    gy_count = lax.axis_size("gy")
    y_total = y_part * gx_count
    norm_factor = 1.0 / (x_total * y_total * z_cells)
    cos_x, sin_x = phase_tables(x_total)
    real_part, imag_part = complex_sum(
        spectrum[0], spectrum[1], cos_x, sin_x, "cazk,kx->cxaz", False
    )
    packed = jnp.stack([real_part, imag_part]).reshape(2, comp_count, 1, x_total, y_part * z_part)
    arrived = lax.all_to_all(packed, "gx", split_axis=3, concat_axis=2, tiled=True)
    count_here = arrived.shape[1]
    pieces = arrived.reshape(2, count_here, gx_count, x_cells, y_part, z_part)
    cos_y, sin_y = phase_tables(y_total)
    cos_y = cos_y.reshape(gx_count, y_part, y_total)
    sin_y = sin_y.reshape(gx_count, y_part, y_total)
    real_out, imag_out = complex_sum(pieces[0], pieces[1], cos_y, sin_y, "cgxaz,gay->cyzx", False)
    middle = jnp.stack([real_out, imag_out]).reshape(2, count_here, 1, y_total, z_part * x_cells)
    arrived = lax.all_to_all(middle, "gy", split_axis=3, concat_axis=2, tiled=True)
    count_here = arrived.shape[1]
    pieces = arrived.reshape(2, count_here, gy_count, y_cells, z_part, x_cells)
    cos_z = cos_back.reshape(gy_count, z_part, z_cells)
    sin_z = sin_back.reshape(gy_count, z_part, z_cells)
    cos_real = contract("cgybx,gbn->cxyn", pieces[0], cos_z)
    sin_imag = contract("cgybx,gbn->cxyn", pieces[1], sin_z)
    return (cos_real - sin_imag) * norm_factor


def shards(velocity, stress, lame_lambda, shear_modulus, buoyancy, source_p, source_s):
    lame_value = lame_lambda.astype(jnp.float32)
    shear_value = shear_modulus.astype(jnp.float32)
    buoy_value = buoyancy.astype(jnp.float32)
    for step_index in range(STEPS):
        stress = stress_step(velocity, stress, lame_value, shear_value)
        velocity = velocity_step(velocity, stress, buoy_value)
    x_cells, y_cells, z_cells = (velocity.shape[1], velocity.shape[2], velocity.shape[3])
    gy_count = lax.axis_size("gy")
    cos_fwd, sin_fwd, cos_back, sin_back, waves = z_tables(z_cells, gy_count)
    spectra = forward(velocity, cos_fwd, sin_fwd)
    compression = project(spectra, waves, z_cells)
    p_field = inverse_fields(compression, x_cells, y_cells, z_cells, cos_back, sin_back)
    s_field = velocity - p_field
    image_p = jnp.sum(source_p.astype(jnp.float32) * p_field, axis=0)
    image_s = jnp.sum(source_s.astype(jnp.float32) * s_field, axis=0)
    return (image_p, image_s)


def solution(mesh):
    in_specs = (
        P(None, "gx", "gy", None),
        P(None, "gx", "gy", None),
        P("gx", "gy", None),
        P("gx", "gy", None),
        P("gx", "gy", None),
        P(None, "gx", "gy", None),
        P(None, "gx", "gy", None),
    )
    out_specs = (P("gx", "gy", None), P("gx", "gy", None))
    return jax.shard_map(shards, mesh=mesh, in_specs=in_specs, out_specs=out_specs, check_vma=False)
```

profile of v0, /device:TPU:64, one launch (start us, length us, event | category | flops | bytes accessed | tf_op | source)
XLA Modules:
  0.0 321.7 jit_solution(4998562081433264974)
XLA Ops:
  1.8 10.0 %collective-permute-start.1 = (f32[1,8,1,128]{3,1,2,0:T(8,128)S(1)}, f32[1,8,1,128]{3,1,2,0:T(8,128)S(1)}, u32[]{:S(2)}, u32[]{:S(2)}) collective-permute-start(f32[1,8,1,128]{3,1,2,0:T(8,128)S(1)} %bitcast.460), channel_id=1, source_target_pairs={{0,1},{1,2},{2,3},{3,4},{4,5},{5,6},{6,7},{8,9},{9,10},{10,11},{11... | collective-permute-start | bytes 12296 | tf_op jit(solution)/shard_map/ppermute | solution.py:14
  22.4 6.9 %collective-permute-done.3 = f32[2,8,1,128]{3,1,2,0:T(8,128)S(1)} collective-permute-done((f32[2,8,1,128]{3,1,2,0:T(8,128)S(1)}, f32[2,8,1,128]{3,1,2,0:T(8,128)S(1)}, u32[]{:S(2)}, u32[]{:S(2)}) %collective-permute-start.3) | collective-permute-done | bytes 8224 | tf_op jit(solution)/shard_map/ppermute | solution.py:14
  35.1 5.8 %collective-permute-start.2 = (f32[1,1,32,128]{3,2,1,0:T(8,128)S(1)}, f32[1,1,32,128]{3,2,1,0:T(8,128)S(1)}, u32[]{:S(2)}, u32[]{:S(2)}) collective-permute-start(f32[1,1,32,128]{3,2,1,0:T(8,128)S(1)} %slice_bitcast_fusion.28), channel_id=1, source_target_pairs={{8,0},{16,8},{24,16},{32,24},{40,32},{48,40},{56,48},{64,56},{72,6... | collective-permute-start | bytes 49160 | tf_op jit(solution)/shard_map/ppermute | solution.py:14
  43.8 6.4 %collective-permute-done.8 = f32[1,8,1,128]{3,1,2,0:T(8,128)S(1)} collective-permute-done((f32[1,8,1,128]{3,1,2,0:T(8,128)S(1)}, f32[1,8,1,128]{3,1,2,0:T(8,128)S(1)}, u32[]{:S(2)}, u32[]{:S(2)}) %collective-permute-start.8) | collective-permute-done | bytes 4128 | tf_op jit(solution)/shard_map/ppermute | solution.py:14
  52.6 8.5 %collective-permute-start.9 = (f32[1,8,1,128]{3,1,2,0:T(8,128)S(1)}, f32[1,8,1,128]{3,1,2,0:T(8,128)S(1)}, u32[]{:S(2)}, u32[]{:S(2)}) collective-permute-start(f32[1,8,1,128]{3,1,2,0:T(8,128)S(1)} %bitcast.461), channel_id=1, source_target_pairs={{0,1},{1,2},{2,3},{3,4},{4,5},{5,6},{6,7},{8,9},{9,10},{10,11},{11... | collective-permute-start | bytes 12296 | tf_op jit(solution)/shard_map/ppermute | solution.py:14
  63.3 5.0 %collective-permute-done.6 = f32[1,1,32,128]{3,2,1,0:T(8,128)S(1)} collective-permute-done((f32[1,1,32,128]{3,2,1,0:T(8,128)S(1)}, f32[1,1,32,128]{3,2,1,0:T(8,128)S(1)}, u32[]{:S(2)}, u32[]{:S(2)}) %collective-permute-start.6) | collective-permute-done | bytes 16416 | tf_op jit(solution)/shard_map/ppermute | solution.py:14
  68.7 5.6 %collective-permute-start.13 = (f32[2,8,1,128]{3,1,2,0:T(8,128)S(1)}, f32[2,8,1,128]{3,1,2,0:T(8,128)S(1)}, u32[]{:S(2)}, u32[]{:S(2)}) collective-permute-start(f32[2,8,1,128]{3,1,2,0:T(8,128)S(1)} %pad_maximum_fusion.15), channel_id=1, source_target_pairs={{0,1},{1,2},{2,3},{3,4},{4,5},{5,6},{6,7},{8,9},{9,10},{10,11},{11... | collective-permute-start | bytes 24584 | tf_op jit(solution)/shard_map/ppermute | solution.py:14
  77.8 5.8 %collective-permute-start.10 = (f32[1,1,32,128]{3,2,1,0:T(8,128)S(1)}, f32[1,1,32,128]{3,2,1,0:T(8,128)S(1)}, u32[]{:S(2)}, u32[]{:S(2)}) collective-permute-start(f32[1,1,32,128]{3,2,1,0:T(8,128)S(1)} %slice_bitcast_fusion.20), channel_id=1, source_target_pairs={{8,0},{16,8},{24,16},{32,24},{40,32},{48,40},{56,48},{64,56},{72,6... | collective-permute-start | bytes 49160 | tf_op jit(solution)/shard_map/ppermute | solution.py:14
  89.0 8.9 %all-to-all-start = ((f32[2,3,1,72,256]{4,0,2,1,3:T(2,128)}), f32[2,3,1,72,256]{4,0,2,1,3:T(2,128)S(1)}, u32[]{:S(2)}, u32[]{:S(2)}) async-start(f32[2,3,1,72,256]{4,0,2,1,3:T(2,128)} %pad_maximum_fusion.2), calls=%async_computation | async-start | bytes 884736 | tf_op jit(solution)/shard_map/all_to_all | solution.py:159
  98.0 14.3 %all-to-all-done = f32[2,3,1,72,256]{4,0,2,1,3:T(2,128)S(1)} async-done(((f32[2,3,1,72,256]{4,0,2,1,3:T(2,128)}), f32[2,3,1,72,256]{4,0,2,1,3:T(2,128)S(1)}, u32[]{:S(2)}, u32[]{:S(2)}) %all-to-all-start) | async-done | bytes 442400 | tf_op jit(solution)/shard_map/all_to_all | solution.py:159
  128.2 8.0 %all-to-all-start.1 = ((f32[2,3,1,256,72]{4,2,1,0,3:T(1,128)}), f32[2,3,1,256,72]{4,2,1,0,3:T(1,128)S(1)}, u32[]{:S(2)}, u32[]{:S(2)}) async-start(f32[2,3,1,256,72]{4,2,1,0,3:T(1,128)} %copy.142), calls=%async_computation.1 | async-start | bytes 1572864 | tf_op jit(solution)/shard_map/all_to_all | solution.py:167
  136.4 21.7 %all-to-all-done.1 = f32[2,3,1,256,72]{4,2,1,0,3:T(1,128)S(1)} async-done(((f32[2,3,1,256,72]{4,2,1,0,3:T(1,128)}), f32[2,3,1,256,72]{4,2,1,0,3:T(1,128)S(1)}, u32[]{:S(2)}, u32[]{:S(2)}) %all-to-all-start.1) | async-done | bytes 442400 | tf_op jit(solution)/shard_map/all_to_all | solution.py:167
  164.1 5.4 %copy.146 = f32[3,64,4,9,8]{1,3,4,2,0:T(8,128)S(1)} copy(f32[3,64,4,9,8]{4,3,0,2,1:T(8,128)} %reshape.522) | data formatting | bytes 442368 | tf_op jit(solution)/shard_map/squeeze | solution.py:173
  173.3 5.8 %copy.144 = f32[3,64,4,9,8]{1,3,4,2,0:T(8,128)S(1)} copy(f32[3,64,4,9,8]{4,3,0,2,1:T(8,128)} %reshape.521) | data formatting | bytes 442368 | tf_op jit(solution)/shard_map/squeeze | solution.py:173
  179.1 4.9 %convolution_bitcast_fusion.2 = f32[3,4,9,512]{3,2,1,0:T(8,128)S(1)} fusion(f32[3,64,4,9,8]{1,3,4,2,0:T(8,128)S(1)} %copy.146, s32[64,8]{0,1:T(8,128)S(1)} %multiply_add_fusion), kind=kOutput, calls=%fused_computation.20 | convolution fusion | flops 343408640 | bytes 444416 | tf_op jit(solution)/shard_map/cgazl,glk->cazk/dot_general | solution.py:124
  188.9 5.0 %fusion.49 = f32[1,3,4,9,512]{4,3,2,1,0:T(8,128)S(1)} fusion(f32[3,4,9,512]{3,2,1,0:T(8,128)S(1)} %convolution_bitcast_fusion.2, f32[3,64,4,9,8]{1,3,4,2,0:T(8,128)S(1)} %copy.144, s32[64,8]{0,1:T(8,128)S(1)} %multiply_add_fusion), kind=kOutput, calls=%fused_computation.46 | convolution fusion | flops 343463936 | bytes 665600 | tf_op jit(solution)/shard_map/cgazl,glk->cazk/dot_general | solution.py:124
  199.2 5.1 %fusion.71 = f32[512,3,4,9]{0,3,2,1:T(8,128)S(1)} fusion(f32[2,3,4,9,512]{4,3,2,1,0:T(8,128)S(1)} %pad_maximum_fusion), kind=kOutput, calls=%fused_computation.62 | convolution fusion | flops 343408640 | bytes 614400 | tf_op jit(solution)/shard_map/cazk,kx->cxaz/dot_general | solution.py:124
  204.3 5.3 %fusion.69 = f32[512,3,4,9]{0,3,2,1:T(8,128)S(1)} fusion(f32[2,3,4,9,512]{4,3,2,1,0:T(8,128)S(1)} %pad_maximum_fusion), kind=kOutput, calls=%fused_computation.60 | convolution fusion | flops 343408640 | bytes 614400 | tf_op jit(solution)/shard_map/cazk,kx->cxaz/dot_general | solution.py:124
  209.7 5.2 %fusion.43 = f32[3,512,4,9]{1,3,2,0:T(8,128)S(1)} fusion(f32[512,3,4,9]{0,3,2,1:T(8,128)S(1)} %fusion.71, f32[2,3,4,9,512]{4,3,2,1,0:T(8,128)S(1)} %pad_maximum_fusion), kind=kOutput, calls=%fused_computation.35 | convolution fusion | flops 343463936 | bytes 1007616 | tf_op jit(solution)/shard_map/cazk,kx->cxaz/dot_general | solution.py:124
  215.0 5.2 %fusion.42 = f32[3,512,4,9]{1,3,2,0:T(8,128)S(1)} fusion(f32[512,3,4,9]{0,3,2,1:T(8,128)S(1)} %fusion.69, f32[2,3,4,9,512]{4,3,2,1,0:T(8,128)S(1)} %pad_maximum_fusion), kind=kOutput, calls=%fused_computation.33 | convolution fusion | flops 343463936 | bytes 1007616 | tf_op jit(solution)/shard_map/cazk,kx->cxaz/dot_general | solution.py:124
  225.6 7.6 %all-to-all-start.2 = ((f32[64,1,1728]{2,1,0:T(1,128)}), f32[64,1,1728]{2,1,0:T(1,128)S(1)}, u32[]{:S(2)}, u32[]{:S(2)}) async-start(f32[64,1,1728]{2,1,0:T(1,128)} %reshape.531), calls=%async_computation.2 | async-start | bytes 917504 | tf_op jit(solution)/shard_map/all_to_all | solution.py:211
  233.2 15.2 %all-to-all-done.2 = f32[64,1,1728]{2,1,0:T(1,128)S(1)} async-done(((f32[64,1,1728]{2,1,0:T(1,128)}), f32[64,1,1728]{2,1,0:T(1,128)S(1)}, u32[]{:S(2)}, u32[]{:S(2)}) %all-to-all-start.2) | async-done | bytes 442400 | tf_op jit(solution)/shard_map/all_to_all | solution.py:211
  253.4 6.2 %slice_reduce_fusion.1 = (f32[3,512,36]{2,0,1:T(4,128)}, f32[3,512,36]{2,0,1:T(4,128)}) fusion(f32[2,3,1,512,36]{4,0,2,1,3:T(2,128)S(1)} %bitcast.413), kind=kLoop, calls=%fused_computation.79 | loop fusion | bytes 884736 | tf_op jit(solution)/shard_map/slice | solution.py:217
  287.0 26.1 %all-to-all-done.3 = f32[2,3,1,256,72]{4,2,1,0,3:T(1,128)S(1)} async-done(((f32[2,3,1,256,72]{4,2,1,0,3:T(1,128)}), f32[2,3,1,256,72]{4,2,1,0,3:T(1,128)S(1)}, u32[]{:S(2)}, u32[]{:S(2)}) %all-to-all-start.3) | async-done | bytes 442400 | tf_op jit(solution)/shard_map/all_to_all | solution.py:219
  (176 shorter events, 115.9 us)
Async XLA Ops:
  0.6 28.7 %copy-start = (f32[3,8,32,128]{3,2,1,0:T(8,128)S(1)}, f32[3,8,32,128]{3,2,1,0:T(8,128)}, u32[]{:S(2)}) copy-start(f32[3,8,32,128]{3,2,1,0:T(8,128)} %param.7) | copy-start | bytes 1179652
  0.6 28.7 %copy-start.3 = (bf16[8,32,128]{2,1,0:T(8,128)(2,1)S(1)}, bf16[8,32,128]{2,1,0:T(8,128)(2,1)}, u32[]{:S(2)}) copy-start(bf16[8,32,128]{2,1,0:T(8,128)(2,1)} %param.10) | copy-start | bytes 196612
  0.7 28.7 %copy-start.5 = (f32[6,8,32,128]{3,2,1,0:T(8,128)S(1)}, f32[6,8,32,128]{3,2,1,0:T(8,128)}, u32[]{:S(2)}) copy-start(f32[6,8,32,128]{3,2,1,0:T(8,128)} %param.8) | copy-start | bytes 2359300
  1.8 27.6 %copy-start.6 = (bf16[8,32,128]{2,1,0:T(8,128)(2,1)S(1)}, bf16[8,32,128]{2,1,0:T(8,128)(2,1)}, u32[]{:S(2)}) copy-start(bf16[8,32,128]{2,1,0:T(8,128)(2,1)} %param.9) | copy-start | bytes 196612
  1.8 27.6 %collective-permute-start.1 = (f32[1,8,1,128]{3,1,2,0:T(8,128)S(1)}, f32[1,8,1,128]{3,1,2,0:T(8,128)S(1)}, u32[]{:S(2)}, u32[]{:S(2)}) collective-permute-start(f32[1,8,1,128]{3,1,2,0:T(8,128)S(1)} %bitcast.460), channel_id=1, source_target_pairs={{0,1},{1,2},{2,3},{3,4},{4,5},{5,6},{6,7},{8,9},{9,10},{10,11},{11... | collective-permute-start | bytes 12296 | tf_op jit(solution)/shard_map/ppermute | solution.py:14
  12.6 16.7 %collective-permute-start.4 = (f32[2,1,32,128]{3,2,1,0:T(8,128)S(1)}, f32[2,1,32,128]{3,2,1,0:T(8,128)S(1)}, u32[]{:S(2)}, u32[]{:S(2)}) collective-permute-start(f32[2,1,32,128]{3,2,1,0:T(8,128)S(1)} %stack.134), channel_id=1, source_target_pairs={{8,0},{16,8},{24,16},{32,24},{40,32},{48,40},{56,48},{64,56},{72,6... | collective-permute-start | bytes 98312 | tf_op jit(solution)/shard_map/ppermute | solution.py:14
  17.9 11.6 %collective-permute-start = (f32[1,1,32,128]{3,2,1,0:T(8,128)S(1)}, f32[1,1,32,128]{3,2,1,0:T(8,128)S(1)}, u32[]{:S(2)}, u32[]{:S(2)}) collective-permute-start(f32[1,1,32,128]{3,2,1,0:T(8,128)S(1)} %slice.326), channel_id=1, source_target_pairs={{0,8},{8,16},{16,24},{24,32},{32,40},{40,48},{48,56},{56,64},{64,7... | collective-permute-start | bytes 49160 | tf_op jit(solution)/shard_map/ppermute | solution.py:14
  19.8 9.5 %collective-permute-start.3 = (f32[2,8,1,128]{3,1,2,0:T(8,128)S(1)}, f32[2,8,1,128]{3,1,2,0:T(8,128)S(1)}, u32[]{:S(2)}, u32[]{:S(2)}) collective-permute-start(f32[2,8,1,128]{3,1,2,0:T(8,128)S(1)} %pad_maximum_fusion.12), channel_id=1, source_target_pairs={{1,0},{2,1},{3,2},{4,3},{5,4},{6,5},{7,6},{9,8},{10,9},{11,10},{12... | collective-permute-start | bytes 24584 | tf_op jit(solution)/shard_map/ppermute | solution.py:14
  29.8 12.3 %collective-permute-start.5 = (f32[2,8,1,128]{3,1,2,0:T(8,128)S(1)}, f32[2,8,1,128]{3,1,2,0:T(8,128)S(1)}, u32[]{:S(2)}, u32[]{:S(2)}) collective-permute-start(f32[2,8,1,128]{3,1,2,0:T(8,128)S(1)} %pad_maximum_fusion.13), channel_id=1, source_target_pairs={{0,1},{1,2},{2,3},{3,4},{4,5},{5,6},{6,7},{8,9},{9,10},{10,11},{11... | collective-permute-start | bytes 24584 | tf_op jit(solution)/shard_map/ppermute | solution.py:14
  33.2 9.0 %collective-permute-start.7 = (f32[2,1,32,128]{3,2,1,0:T(8,128)S(1)}, f32[2,1,32,128]{3,2,1,0:T(8,128)S(1)}, u32[]{:S(2)}, u32[]{:S(2)}) collective-permute-start(f32[2,1,32,128]{3,2,1,0:T(8,128)S(1)} %pad_maximum_fusion.9), channel_id=1, source_target_pairs={{0,8},{8,16},{16,24},{24,32},{32,40},{40,48},{48,56},{56,64},{64,7... | collective-permute-start | bytes 98312 | tf_op jit(solution)/shard_map/ppermute | solution.py:14
  35.1 7.2 %collective-permute-start.2 = (f32[1,1,32,128]{3,2,1,0:T(8,128)S(1)}, f32[1,1,32,128]{3,2,1,0:T(8,128)S(1)}, u32[]{:S(2)}, u32[]{:S(2)}) collective-permute-start(f32[1,1,32,128]{3,2,1,0:T(8,128)S(1)} %slice_bitcast_fusion.28), channel_id=1, source_target_pairs={{8,0},{16,8},{24,16},{32,24},{40,32},{48,40},{56,48},{64,56},{72,6... | collective-permute-start | bytes 49160 | tf_op jit(solution)/shard_map/ppermute | solution.py:14
  40.8 9.4 %collective-permute-start.8 = (f32[1,8,1,128]{3,1,2,0:T(8,128)S(1)}, f32[1,8,1,128]{3,1,2,0:T(8,128)S(1)}, u32[]{:S(2)}, u32[]{:S(2)}) collective-permute-start(f32[1,8,1,128]{3,1,2,0:T(8,128)S(1)} %bitcast.459), channel_id=1, source_target_pairs={{1,0},{2,1},{3,2},{4,3},{5,4},{6,5},{7,6},{9,8},{10,9},{11,10},{12... | collective-permute-start | bytes 12296 | tf_op jit(solution)/shard_map/ppermute | solution.py:14
  42.5 20.7 %collective-permute-start.11 = (f32[2,8,1,128]{3,1,2,0:T(8,128)S(1)}, f32[2,8,1,128]{3,1,2,0:T(8,128)S(1)}, u32[]{:S(2)}, u32[]{:S(2)}) collective-permute-start(f32[2,8,1,128]{3,1,2,0:T(8,128)S(1)} %pad_maximum_fusion.14), channel_id=1, source_target_pairs={{1,0},{2,1},{3,2},{4,3},{5,4},{6,5},{7,6},{9,8},{10,9},{11,10},{12... | collective-permute-start | bytes 24584 | tf_op jit(solution)/shard_map/ppermute | solution.py:14
  50.7 12.6 %collective-permute-start.12 = (f32[2,1,32,128]{3,2,1,0:T(8,128)S(1)}, f32[2,1,32,128]{3,2,1,0:T(8,128)S(1)}, u32[]{:S(2)}, u32[]{:S(2)}) collective-permute-start(f32[2,1,32,128]{3,2,1,0:T(8,128)S(1)} %pad_maximum_fusion.10), channel_id=1, source_target_pairs={{8,0},{16,8},{24,16},{32,24},{40,32},{48,40},{56,48},{64,56},{72,6... | collective-permute-start | bytes 98312 | tf_op jit(solution)/shard_map/ppermute | solution.py:14
  52.6 10.7 %collective-permute-start.9 = (f32[1,8,1,128]{3,1,2,0:T(8,128)S(1)}, f32[1,8,1,128]{3,1,2,0:T(8,128)S(1)}, u32[]{:S(2)}, u32[]{:S(2)}) collective-permute-start(f32[1,8,1,128]{3,1,2,0:T(8,128)S(1)} %bitcast.461), channel_id=1, source_target_pairs={{0,1},{1,2},{2,3},{3,4},{4,5},{5,6},{6,7},{8,9},{9,10},{10,11},{11... | collective-permute-start | bytes 12296 | tf_op jit(solution)/shard_map/ppermute | solution.py:14
  61.1 7.2 %collective-permute-start.6 = (f32[1,1,32,128]{3,2,1,0:T(8,128)S(1)}, f32[1,1,32,128]{3,2,1,0:T(8,128)S(1)}, u32[]{:S(2)}, u32[]{:S(2)}) collective-permute-start(f32[1,1,32,128]{3,2,1,0:T(8,128)S(1)} %slice_bitcast_fusion.25), channel_id=1, source_target_pairs={{0,8},{8,16},{16,24},{24,32},{32,40},{40,48},{48,56},{56,64},{64,7... | collective-permute-start | bytes 49160 | tf_op jit(solution)/shard_map/ppermute | solution.py:14
  68.7 14.8 %collective-permute-start.13 = (f32[2,8,1,128]{3,1,2,0:T(8,128)S(1)}, f32[2,8,1,128]{3,1,2,0:T(8,128)S(1)}, u32[]{:S(2)}, u32[]{:S(2)}) collective-permute-start(f32[2,8,1,128]{3,1,2,0:T(8,128)S(1)} %pad_maximum_fusion.15), channel_id=1, source_target_pairs={{0,1},{1,2},{2,3},{3,4},{4,5},{5,6},{6,7},{8,9},{9,10},{10,11},{11... | collective-permute-start | bytes 24584 | tf_op jit(solution)/shard_map/ppermute | solution.py:14
  74.4 9.1 %collective-permute-start.14 = (f32[2,1,32,128]{3,2,1,0:T(8,128)S(1)}, f32[2,1,32,128]{3,2,1,0:T(8,128)S(1)}, u32[]{:S(2)}, u32[]{:S(2)}) collective-permute-start(f32[2,1,32,128]{3,2,1,0:T(8,128)S(1)} %pad_maximum_fusion.11), channel_id=1, source_target_pairs={{0,8},{8,16},{16,24},{24,32},{32,40},{40,48},{48,56},{56,64},{64,7... | collective-permute-start | bytes 98312 | tf_op jit(solution)/shard_map/ppermute | solution.py:14
  76.4 9.4 %collective-permute-start.15 = (f32[1,8,1,128]{3,1,2,0:T(8,128)S(1)}, f32[1,8,1,128]{3,1,2,0:T(8,128)S(1)}, u32[]{:S(2)}, u32[]{:S(2)}) collective-permute-start(f32[1,8,1,128]{3,1,2,0:T(8,128)S(1)} %bitcast.462), channel_id=1, source_target_pairs={{1,0},{2,1},{3,2},{4,3},{5,4},{6,5},{7,6},{9,8},{10,9},{11,10},{12... | collective-permute-start | bytes 12296 | tf_op jit(solution)/shard_map/ppermute | solution.py:14
  77.8 8.1 %collective-permute-start.10 = (f32[1,1,32,128]{3,2,1,0:T(8,128)S(1)}, f32[1,1,32,128]{3,2,1,0:T(8,128)S(1)}, u32[]{:S(2)}, u32[]{:S(2)}) collective-permute-start(f32[1,1,32,128]{3,2,1,0:T(8,128)S(1)} %slice_bitcast_fusion.20), channel_id=1, source_target_pairs={{8,0},{16,8},{24,16},{32,24},{40,32},{48,40},{56,48},{64,56},{72,6... | collective-permute-start | bytes 49160 | tf_op jit(solution)/shard_map/ppermute | solution.py:14
  89.0 23.3 %all-to-all-start = ((f32[2,3,1,72,256]{4,0,2,1,3:T(2,128)}), f32[2,3,1,72,256]{4,0,2,1,3:T(2,128)S(1)}, u32[]{:S(2)}, u32[]{:S(2)}) async-start(f32[2,3,1,72,256]{4,0,2,1,3:T(2,128)} %pad_maximum_fusion.2), calls=%async_computation | async-start | bytes 884736 | tf_op jit(solution)/shard_map/all_to_all | solution.py:159
  128.2 29.9 %all-to-all-start.1 = ((f32[2,3,1,256,72]{4,2,1,0,3:T(1,128)}), f32[2,3,1,256,72]{4,2,1,0,3:T(1,128)S(1)}, u32[]{:S(2)}, u32[]{:S(2)}) async-start(f32[2,3,1,256,72]{4,2,1,0,3:T(1,128)} %copy.142), calls=%async_computation.1 | async-start | bytes 1572864 | tf_op jit(solution)/shard_map/all_to_all | solution.py:167
  225.6 22.8 %all-to-all-start.2 = ((f32[64,1,1728]{2,1,0:T(1,128)}), f32[64,1,1728]{2,1,0:T(1,128)S(1)}, u32[]{:S(2)}, u32[]{:S(2)}) async-start(f32[64,1,1728]{2,1,0:T(1,128)} %reshape.531), calls=%async_computation.2 | async-start | bytes 917504 | tf_op jit(solution)/shard_map/all_to_all | solution.py:211
  283.2 29.9 %all-to-all-start.3 = ((f32[2,3,1,256,72]{4,2,1,0,3:T(1,128)}), f32[2,3,1,256,72]{4,2,1,0,3:T(1,128)S(1)}, u32[]{:S(2)}, u32[]{:S(2)}) async-start(f32[2,3,1,256,72]{4,2,1,0,3:T(1,128)} %copy.160), calls=%async_computation.3 | async-start | bytes 1572864 | tf_op jit(solution)/shard_map/all_to_all | solution.py:219
  (5 other events, 29.9 us)
where the time goes:
time: 327 us; the launch traced here: 322 us
  waiting for transfers between devices  97.8 us (30%)
  starting transfers between devices  86.4 us (26%)
  matrix products  69.8 us (21%)
  local copies, waits for them, and re-layouts  60.5 us (19%)
  other arithmetic  5.12 us (2%)
    dot_general x20, matrix products, contract(): return jnp.einsum(pattern, left, right, precision=lax.Precision.HIGHEST)  69.8 us
    ppermute x16, starting transfers between devices, passed_along(): return lax.ppermute(block, axis, route)  58.2 us
    all_to_all x1, waiting for transfers between devices, inverse_fields(): lax.all_to_all(middle, 'gy', split_axis=3, concat_axis=2, tiled=True)  26.1 us
    all_to_all x1, waiting for transfers between devices, forward(): lax.all_to_all(after_y, 'gx', split_axis=3, concat_axis=2, tiled=True)  21.7 us
    ppermute x16, waiting for transfers between devices, passed_along(): return lax.ppermute(block, axis, route)  20.6 us
    all_to_all x1, waiting for transfers between devices, inverse_fields(): lax.all_to_all(packed, 'gx', split_axis=3, concat_axis=2, tiled=True)  15.2 us
    all_to_all x1, waiting for transfers between devices, forward(): lax.all_to_all(packed, 'gy', split_axis=3, concat_axis=2, tiled=True)  14.3 us
    squeeze x3, local copies, waits for them, and re-layouts, forward(): pieces[0]  9.83 us
  transfers between devices with their start and end apart: 20, of which 9 were waited for; matrix products, arithmetic and copies ran while one was open for 1% of the time, Pallas kernels for 0%

commit v1 on v0

--- a/solution.py
+++ b/solution.py
@@ -216,7 +216,10 @@
     sin_y = sin_y.reshape(gx_count, y_part, y_total)
     real_out, imag_out = complex_sum(pieces[0], pieces[1], cos_y, sin_y, "cgxaz,gay->cyzx", False)
     middle = jnp.stack([real_out, imag_out]).reshape(2, count_here, 1, y_total, z_part * x_cells)
-    arrived = lax.all_to_all(middle, "gy", split_axis=3, concat_axis=2, tiled=True)
+    arrived = jnp.concatenate(
+        lax.all_to_all(jnp.stack(jnp.split(middle, lax.axis_size("gy"), axis=3)), "gy", 0, 0),
+        axis=2,
+    )
     count_here = arrived.shape[1]
     pieces = arrived.reshape(2, count_here, gy_count, y_cells, z_part, x_cells)
     cos_z = cos_back.reshape(gy_count, z_part, z_cells)

time: 327 us -> 331 us (1.012)
  local copies, waits for them, and re-layouts: 60.5 us -> 63.9 us
    unnamed x20 -> x27, local copies, waits for them, and re-layouts: 6.72 us -> 11.3 us
    slice x4 -> x1, local copies, waits for them, and re-layouts: 7.3 us -> 6.2 us  [inverse_fields(): pieces[1]]
where the time goes in v1:
time: 331 us; the launch traced here: 325 us
  waiting for transfers between devices  97.8 us (30%)
  starting transfers between devices  86.4 us (26%)
  matrix products  69.4 us (21%)
  local copies, waits for them, and re-layouts  63.9 us (19%)
  other arithmetic  5.51 us (2%)
    dot_general x20, matrix products, contract(): return jnp.einsum(pattern, left, right, precision=lax.Precision.HIGHEST)  69.4 us
    ppermute x16, starting transfers between devices, passed_along(): return lax.ppermute(block, axis, route)  58.2 us
    all_to_all x1, waiting for transfers between devices, inverse_fields(): lax.all_to_all(jnp.stack(jnp.split(middle, lax.axis_size('gy'), axis=3)),...  26.1 us
    all_to_all x1, waiting for transfers between devices, forward(): lax.all_to_all(after_y, 'gx', split_axis=3, concat_axis=2, tiled=True)  21.7 us
    ppermute x16, waiting for transfers between devices, passed_along(): return lax.ppermute(block, axis, route)  20.6 us
    all_to_all x1, waiting for transfers between devices, inverse_fields(): lax.all_to_all(packed, 'gx', split_axis=3, concat_axis=2, tiled=True)  15.2 us
    all_to_all x1, waiting for transfers between devices, forward(): lax.all_to_all(packed, 'gy', split_axis=3, concat_axis=2, tiled=True)  14.3 us
    unnamed x27, local copies, waits for them, and re-layouts  11.3 us
  transfers between devices with their start and end apart: 20, of which 9 were waited for; matrix products, arithmetic and copies ran while one was open for 1% of the time, Pallas kernels for 0%

profile of v1, /device:TPU:64, one launch (start us, length us, event | category | flops | bytes accessed | tf_op | source)
XLA Modules:
  0.0 325.2 jit_solution(3533298656468392771)
XLA Ops:
  1.8 10.0 %collective-permute-start.1 = (f32[1,8,1,128]{3,1,2,0:T(8,128)S(1)}, f32[1,8,1,128]{3,1,2,0:T(8,128)S(1)}, u32[]{:S(2)}, u32[]{:S(2)}) collective-permute-start(f32[1,8,1,128]{3,1,2,0:T(8,128)S(1)} %bitcast.474), channel_id=1, source_target_pairs={{0,1},{1,2},{2,3},{3,4},{4,5},{5,6},{6,7},{8,9},{9,10},{10,11},{11... | collective-permute-start | bytes 12296 | tf_op jit(solution)/shard_map/ppermute | solution.py:14
  22.4 6.9 %collective-permute-done.3 = f32[2,8,1,128]{3,1,2,0:T(8,128)S(1)} collective-permute-done((f32[2,8,1,128]{3,1,2,0:T(8,128)S(1)}, f32[2,8,1,128]{3,1,2,0:T(8,128)S(1)}, u32[]{:S(2)}, u32[]{:S(2)}) %collective-permute-start.3) | collective-permute-done | bytes 8224 | tf_op jit(solution)/shard_map/ppermute | solution.py:14
  35.1 5.8 %collective-permute-start.2 = (f32[1,1,32,128]{3,2,1,0:T(8,128)S(1)}, f32[1,1,32,128]{3,2,1,0:T(8,128)S(1)}, u32[]{:S(2)}, u32[]{:S(2)}) collective-permute-start(f32[1,1,32,128]{3,2,1,0:T(8,128)S(1)} %slice_bitcast_fusion.30), channel_id=1, source_target_pairs={{8,0},{16,8},{24,16},{32,24},{40,32},{48,40},{56,48},{64,56},{72,6... | collective-permute-start | bytes 49160 | tf_op jit(solution)/shard_map/ppermute | solution.py:14
  43.8 6.4 %collective-permute-done.8 = f32[1,8,1,128]{3,1,2,0:T(8,128)S(1)} collective-permute-done((f32[1,8,1,128]{3,1,2,0:T(8,128)S(1)}, f32[1,8,1,128]{3,1,2,0:T(8,128)S(1)}, u32[]{:S(2)}, u32[]{:S(2)}) %collective-permute-start.8) | collective-permute-done | bytes 4128 | tf_op jit(solution)/shard_map/ppermute | solution.py:14
  52.6 8.5 %collective-permute-start.9 = (f32[1,8,1,128]{3,1,2,0:T(8,128)S(1)}, f32[1,8,1,128]{3,1,2,0:T(8,128)S(1)}, u32[]{:S(2)}, u32[]{:S(2)}) collective-permute-start(f32[1,8,1,128]{3,1,2,0:T(8,128)S(1)} %bitcast.475), channel_id=1, source_target_pairs={{0,1},{1,2},{2,3},{3,4},{4,5},{5,6},{6,7},{8,9},{9,10},{10,11},{11... | collective-permute-start | bytes 12296 | tf_op jit(solution)/shard_map/ppermute | solution.py:14
  63.3 5.0 %collective-permute-done.6 = f32[1,1,32,128]{3,2,1,0:T(8,128)S(1)} collective-permute-done((f32[1,1,32,128]{3,2,1,0:T(8,128)S(1)}, f32[1,1,32,128]{3,2,1,0:T(8,128)S(1)}, u32[]{:S(2)}, u32[]{:S(2)}) %collective-permute-start.6) | collective-permute-done | bytes 16416 | tf_op jit(solution)/shard_map/ppermute | solution.py:14
  68.7 5.6 %collective-permute-start.13 = (f32[2,8,1,128]{3,1,2,0:T(8,128)S(1)}, f32[2,8,1,128]{3,1,2,0:T(8,128)S(1)}, u32[]{:S(2)}, u32[]{:S(2)}) collective-permute-start(f32[2,8,1,128]{3,1,2,0:T(8,128)S(1)} %pad_maximum_fusion.15), channel_id=1, source_target_pairs={{0,1},{1,2},{2,3},{3,4},{4,5},{5,6},{6,7},{8,9},{9,10},{10,11},{11... | collective-permute-start | bytes 24584 | tf_op jit(solution)/shard_map/ppermute | solution.py:14
  77.8 5.8 %collective-permute-start.10 = (f32[1,1,32,128]{3,2,1,0:T(8,128)S(1)}, f32[1,1,32,128]{3,2,1,0:T(8,128)S(1)}, u32[]{:S(2)}, u32[]{:S(2)}) collective-permute-start(f32[1,1,32,128]{3,2,1,0:T(8,128)S(1)} %slice_bitcast_fusion.22), channel_id=1, source_target_pairs={{8,0},{16,8},{24,16},{32,24},{40,32},{48,40},{56,48},{64,56},{72,6... | collective-permute-start | bytes 49160 | tf_op jit(solution)/shard_map/ppermute | solution.py:14
  89.0 8.9 %all-to-all-start = ((f32[2,3,1,72,256]{4,0,2,1,3:T(2,128)}), f32[2,3,1,72,256]{4,0,2,1,3:T(2,128)S(1)}, u32[]{:S(2)}, u32[]{:S(2)}) async-start(f32[2,3,1,72,256]{4,0,2,1,3:T(2,128)} %pad_maximum_fusion.2), calls=%async_computation | async-start | bytes 884736 | tf_op jit(solution)/shard_map/all_to_all | solution.py:159
  98.0 14.3 %all-to-all-done = f32[2,3,1,72,256]{4,0,2,1,3:T(2,128)S(1)} async-done(((f32[2,3,1,72,256]{4,0,2,1,3:T(2,128)}), f32[2,3,1,72,256]{4,0,2,1,3:T(2,128)S(1)}, u32[]{:S(2)}, u32[]{:S(2)}) %all-to-all-start) | async-done | bytes 442400 | tf_op jit(solution)/shard_map/all_to_all | solution.py:159
  128.2 8.0 %all-to-all-start.1 = ((f32[2,3,1,256,72]{4,2,1,0,3:T(1,128)}), f32[2,3,1,256,72]{4,2,1,0,3:T(1,128)S(1)}, u32[]{:S(2)}, u32[]{:S(2)}) async-start(f32[2,3,1,256,72]{4,2,1,0,3:T(1,128)} %copy.164), calls=%async_computation.1 | async-start | bytes 1572864 | tf_op jit(solution)/shard_map/all_to_all | solution.py:167
  136.4 21.7 %all-to-all-done.1 = f32[2,3,1,256,72]{4,2,1,0,3:T(1,128)S(1)} async-done(((f32[2,3,1,256,72]{4,2,1,0,3:T(1,128)}), f32[2,3,1,256,72]{4,2,1,0,3:T(1,128)S(1)}, u32[]{:S(2)}, u32[]{:S(2)}) %all-to-all-start.1) | async-done | bytes 442400 | tf_op jit(solution)/shard_map/all_to_all | solution.py:167
  164.2 5.4 %copy.168 = f32[3,64,4,9,8]{1,3,4,2,0:T(8,128)S(1)} copy(f32[3,64,4,9,8]{4,3,0,2,1:T(8,128)} %reshape.519) | data formatting | bytes 442368 | tf_op jit(solution)/shard_map/squeeze | solution.py:173
  173.3 5.8 %copy.166 = f32[3,64,4,9,8]{1,3,4,2,0:T(8,128)S(1)} copy(f32[3,64,4,9,8]{4,3,0,2,1:T(8,128)} %reshape.518) | data formatting | bytes 442368 | tf_op jit(solution)/shard_map/squeeze | solution.py:173
  179.1 4.9 %convolution_bitcast_fusion.2 = f32[3,4,9,512]{3,2,1,0:T(8,128)S(1)} fusion(f32[3,64,4,9,8]{1,3,4,2,0:T(8,128)S(1)} %copy.168, s32[64,8]{0,1:T(8,128)S(1)} %multiply_add_fusion), kind=kOutput, calls=%fused_computation.20 | convolution fusion | flops 343408640 | bytes 444416 | tf_op jit(solution)/shard_map/cgazl,glk->cazk/dot_general | solution.py:124
  188.9 5.0 %fusion.49 = f32[1,3,4,9,512]{4,3,2,1,0:T(8,128)S(1)} fusion(f32[3,4,9,512]{3,2,1,0:T(8,128)S(1)} %convolution_bitcast_fusion.2, f32[3,64,4,9,8]{1,3,4,2,0:T(8,128)S(1)} %copy.166, s32[64,8]{0,1:T(8,128)S(1)} %multiply_add_fusion), kind=kOutput, calls=%fused_computation.46 | convolution fusion | flops 343463936 | bytes 665600 | tf_op jit(solution)/shard_map/cgazl,glk->cazk/dot_general | solution.py:124
  199.2 5.1 %fusion.71 = f32[512,3,4,9]{0,3,2,1:T(8,128)S(1)} fusion(f32[2,3,4,9,512]{4,3,2,1,0:T(8,128)S(1)} %pad_maximum_fusion), kind=kOutput, calls=%fused_computation.62 | convolution fusion | flops 343408640 | bytes 614400 | tf_op jit(solution)/shard_map/cazk,kx->cxaz/dot_general | solution.py:124
  204.3 5.3 %fusion.69 = f32[512,3,4,9]{0,3,2,1:T(8,128)S(1)} fusion(f32[2,3,4,9,512]{4,3,2,1,0:T(8,128)S(1)} %pad_maximum_fusion), kind=kOutput, calls=%fused_computation.60 | convolution fusion | flops 343408640 | bytes 614400 | tf_op jit(solution)/shard_map/cazk,kx->cxaz/dot_general | solution.py:124
  209.7 5.2 %fusion.43 = f32[3,512,4,9]{1,3,2,0:T(8,128)S(1)} fusion(f32[512,3,4,9]{0,3,2,1:T(8,128)S(1)} %fusion.71, f32[2,3,4,9,512]{4,3,2,1,0:T(8,128)S(1)} %pad_maximum_fusion), kind=kOutput, calls=%fused_computation.35 | convolution fusion | flops 343463936 | bytes 1007616 | tf_op jit(solution)/shard_map/cazk,kx->cxaz/dot_general | solution.py:124
  215.0 5.2 %fusion.42 = f32[3,512,4,9]{1,3,2,0:T(8,128)S(1)} fusion(f32[512,3,4,9]{0,3,2,1:T(8,128)S(1)} %fusion.69, f32[2,3,4,9,512]{4,3,2,1,0:T(8,128)S(1)} %pad_maximum_fusion), kind=kOutput, calls=%fused_computation.33 | convolution fusion | flops 343463936 | bytes 1007616 | tf_op jit(solution)/shard_map/cazk,kx->cxaz/dot_general | solution.py:124
  225.6 7.6 %all-to-all-start.2 = ((f32[64,1,1728]{2,1,0:T(1,128)}), f32[64,1,1728]{2,1,0:T(1,128)S(1)}, u32[]{:S(2)}, u32[]{:S(2)}) async-start(f32[64,1,1728]{2,1,0:T(1,128)} %reshape.528), calls=%async_computation.2 | async-start | bytes 917504 | tf_op jit(solution)/shard_map/all_to_all | solution.py:211
  233.2 15.2 %all-to-all-done.2 = f32[64,1,1728]{2,1,0:T(1,128)S(1)} async-done(((f32[64,1,1728]{2,1,0:T(1,128)}), f32[64,1,1728]{2,1,0:T(1,128)S(1)}, u32[]{:S(2)}, u32[]{:S(2)}) %all-to-all-start.2) | async-done | bytes 442400 | tf_op jit(solution)/shard_map/all_to_all | solution.py:211
  253.5 6.2 %slice_reduce_fusion = (f32[3,512,36]{2,0,1:T(4,128)}, f32[3,512,36]{2,0,1:T(4,128)}) fusion(f32[2,3,1,512,36]{4,0,2,1,3:T(2,128)S(1)} %bitcast.427), kind=kLoop, calls=%fused_computation.94 | loop fusion | bytes 884736 | tf_op jit(solution)/shard_map/slice | solution.py:217
  291.8 26.1 %all-to-all-done.3 = f32[8,2,3,1,32,72]{5,4,3,2,1,0:T(8,128)S(1)} async-done(((f32[8,2,3,1,32,72]{5,4,3,2,1,0:T(8,128)}), f32[8,2,3,1,32,72]{5,4,3,2,1,0:T(8,128)S(1)}, u32[]{:S(2)}, u32[]{:S(2)}) %all-to-all-start.3) | async-done | bytes 442400 | tf_op jit(solution)/shard_map/all_to_all | solution.py:220
  (188 shorter events, 119.3 us)
Async XLA Ops:
  0.6 28.7 %copy-start = (f32[3,8,32,128]{3,2,1,0:T(8,128)S(1)}, f32[3,8,32,128]{3,2,1,0:T(8,128)}, u32[]{:S(2)}) copy-start(f32[3,8,32,128]{3,2,1,0:T(8,128)} %param.7) | copy-start | bytes 1179652
  0.6 28.7 %copy-start.3 = (bf16[8,32,128]{2,1,0:T(8,128)(2,1)S(1)}, bf16[8,32,128]{2,1,0:T(8,128)(2,1)}, u32[]{:S(2)}) copy-start(bf16[8,32,128]{2,1,0:T(8,128)(2,1)} %param.10) | copy-start | bytes 196612
  0.7 28.7 %copy-start.5 = (f32[6,8,32,128]{3,2,1,0:T(8,128)S(1)}, f32[6,8,32,128]{3,2,1,0:T(8,128)}, u32[]{:S(2)}) copy-start(f32[6,8,32,128]{3,2,1,0:T(8,128)} %param.8) | copy-start | bytes 2359300
  1.8 27.6 %copy-start.6 = (bf16[8,32,128]{2,1,0:T(8,128)(2,1)S(1)}, bf16[8,32,128]{2,1,0:T(8,128)(2,1)}, u32[]{:S(2)}) copy-start(bf16[8,32,128]{2,1,0:T(8,128)(2,1)} %param.9) | copy-start | bytes 196612
  1.8 27.6 %collective-permute-start.1 = (f32[1,8,1,128]{3,1,2,0:T(8,128)S(1)}, f32[1,8,1,128]{3,1,2,0:T(8,128)S(1)}, u32[]{:S(2)}, u32[]{:S(2)}) collective-permute-start(f32[1,8,1,128]{3,1,2,0:T(8,128)S(1)} %bitcast.474), channel_id=1, source_target_pairs={{0,1},{1,2},{2,3},{3,4},{4,5},{5,6},{6,7},{8,9},{9,10},{10,11},{11... | collective-permute-start | bytes 12296 | tf_op jit(solution)/shard_map/ppermute | solution.py:14
  12.6 16.7 %collective-permute-start.4 = (f32[2,1,32,128]{3,2,1,0:T(8,128)S(1)}, f32[2,1,32,128]{3,2,1,0:T(8,128)S(1)}, u32[]{:S(2)}, u32[]{:S(2)}) collective-permute-start(f32[2,1,32,128]{3,2,1,0:T(8,128)S(1)} %stack.161), channel_id=1, source_target_pairs={{8,0},{16,8},{24,16},{32,24},{40,32},{48,40},{56,48},{64,56},{72,6... | collective-permute-start | bytes 98312 | tf_op jit(solution)/shard_map/ppermute | solution.py:14
  17.9 11.6 %collective-permute-start = (f32[1,1,32,128]{3,2,1,0:T(8,128)S(1)}, f32[1,1,32,128]{3,2,1,0:T(8,128)S(1)}, u32[]{:S(2)}, u32[]{:S(2)}) collective-permute-start(f32[1,1,32,128]{3,2,1,0:T(8,128)S(1)} %slice.325), channel_id=1, source_target_pairs={{0,8},{8,16},{16,24},{24,32},{32,40},{40,48},{48,56},{56,64},{64,7... | collective-permute-start | bytes 49160 | tf_op jit(solution)/shard_map/ppermute | solution.py:14
  19.8 9.5 %collective-permute-start.3 = (f32[2,8,1,128]{3,1,2,0:T(8,128)S(1)}, f32[2,8,1,128]{3,1,2,0:T(8,128)S(1)}, u32[]{:S(2)}, u32[]{:S(2)}) collective-permute-start(f32[2,8,1,128]{3,1,2,0:T(8,128)S(1)} %pad_maximum_fusion.12), channel_id=1, source_target_pairs={{1,0},{2,1},{3,2},{4,3},{5,4},{6,5},{7,6},{9,8},{10,9},{11,10},{12... | collective-permute-start | bytes 24584 | tf_op jit(solution)/shard_map/ppermute | solution.py:14
  29.8 12.3 %collective-permute-start.5 = (f32[2,8,1,128]{3,1,2,0:T(8,128)S(1)}, f32[2,8,1,128]{3,1,2,0:T(8,128)S(1)}, u32[]{:S(2)}, u32[]{:S(2)}) collective-permute-start(f32[2,8,1,128]{3,1,2,0:T(8,128)S(1)} %pad_maximum_fusion.13), channel_id=1, source_target_pairs={{0,1},{1,2},{2,3},{3,4},{4,5},{5,6},{6,7},{8,9},{9,10},{10,11},{11... | collective-permute-start | bytes 24584 | tf_op jit(solution)/shard_map/ppermute | solution.py:14
  33.2 9.0 %collective-permute-start.7 = (f32[2,1,32,128]{3,2,1,0:T(8,128)S(1)}, f32[2,1,32,128]{3,2,1,0:T(8,128)S(1)}, u32[]{:S(2)}, u32[]{:S(2)}) collective-permute-start(f32[2,1,32,128]{3,2,1,0:T(8,128)S(1)} %pad_maximum_fusion.9), channel_id=1, source_target_pairs={{0,8},{8,16},{16,24},{24,32},{32,40},{40,48},{48,56},{56,64},{64,7... | collective-permute-start | bytes 98312 | tf_op jit(solution)/shard_map/ppermute | solution.py:14
  35.1 7.2 %collective-permute-start.2 = (f32[1,1,32,128]{3,2,1,0:T(8,128)S(1)}, f32[1,1,32,128]{3,2,1,0:T(8,128)S(1)}, u32[]{:S(2)}, u32[]{:S(2)}) collective-permute-start(f32[1,1,32,128]{3,2,1,0:T(8,128)S(1)} %slice_bitcast_fusion.30), channel_id=1, source_target_pairs={{8,0},{16,8},{24,16},{32,24},{40,32},{48,40},{56,48},{64,56},{72,6... | collective-permute-start | bytes 49160 | tf_op jit(solution)/shard_map/ppermute | solution.py:14
  40.8 9.4 %collective-permute-start.8 = (f32[1,8,1,128]{3,1,2,0:T(8,128)S(1)}, f32[1,8,1,128]{3,1,2,0:T(8,128)S(1)}, u32[]{:S(2)}, u32[]{:S(2)}) collective-permute-start(f32[1,8,1,128]{3,1,2,0:T(8,128)S(1)} %bitcast.473), channel_id=1, source_target_pairs={{1,0},{2,1},{3,2},{4,3},{5,4},{6,5},{7,6},{9,8},{10,9},{11,10},{12... | collective-permute-start | bytes 12296 | tf_op jit(solution)/shard_map/ppermute | solution.py:14
  42.5 20.7 %collective-permute-start.11 = (f32[2,8,1,128]{3,1,2,0:T(8,128)S(1)}, f32[2,8,1,128]{3,1,2,0:T(8,128)S(1)}, u32[]{:S(2)}, u32[]{:S(2)}) collective-permute-start(f32[2,8,1,128]{3,1,2,0:T(8,128)S(1)} %pad_maximum_fusion.14), channel_id=1, source_target_pairs={{1,0},{2,1},{3,2},{4,3},{5,4},{6,5},{7,6},{9,8},{10,9},{11,10},{12... | collective-permute-start | bytes 24584 | tf_op jit(solution)/shard_map/ppermute | solution.py:14
  50.7 12.6 %collective-permute-start.12 = (f32[2,1,32,128]{3,2,1,0:T(8,128)S(1)}, f32[2,1,32,128]{3,2,1,0:T(8,128)S(1)}, u32[]{:S(2)}, u32[]{:S(2)}) collective-permute-start(f32[2,1,32,128]{3,2,1,0:T(8,128)S(1)} %pad_maximum_fusion.10), channel_id=1, source_target_pairs={{8,0},{16,8},{24,16},{32,24},{40,32},{48,40},{56,48},{64,56},{72,6... | collective-permute-start | bytes 98312 | tf_op jit(solution)/shard_map/ppermute | solution.py:14
  52.6 10.7 %collective-permute-start.9 = (f32[1,8,1,128]{3,1,2,0:T(8,128)S(1)}, f32[1,8,1,128]{3,1,2,0:T(8,128)S(1)}, u32[]{:S(2)}, u32[]{:S(2)}) collective-permute-start(f32[1,8,1,128]{3,1,2,0:T(8,128)S(1)} %bitcast.475), channel_id=1, source_target_pairs={{0,1},{1,2},{2,3},{3,4},{4,5},{5,6},{6,7},{8,9},{9,10},{10,11},{11... | collective-permute-start | bytes 12296 | tf_op jit(solution)/shard_map/ppermute | solution.py:14
  61.1 7.2 %collective-permute-start.6 = (f32[1,1,32,128]{3,2,1,0:T(8,128)S(1)}, f32[1,1,32,128]{3,2,1,0:T(8,128)S(1)}, u32[]{:S(2)}, u32[]{:S(2)}) collective-permute-start(f32[1,1,32,128]{3,2,1,0:T(8,128)S(1)} %slice_bitcast_fusion.27), channel_id=1, source_target_pairs={{0,8},{8,16},{16,24},{24,32},{32,40},{40,48},{48,56},{56,64},{64,7... | collective-permute-start | bytes 49160 | tf_op jit(solution)/shard_map/ppermute | solution.py:14
  68.7 14.8 %collective-permute-start.13 = (f32[2,8,1,128]{3,1,2,0:T(8,128)S(1)}, f32[2,8,1,128]{3,1,2,0:T(8,128)S(1)}, u32[]{:S(2)}, u32[]{:S(2)}) collective-permute-start(f32[2,8,1,128]{3,1,2,0:T(8,128)S(1)} %pad_maximum_fusion.15), channel_id=1, source_target_pairs={{0,1},{1,2},{2,3},{3,4},{4,5},{5,6},{6,7},{8,9},{9,10},{10,11},{11... | collective-permute-start | bytes 24584 | tf_op jit(solution)/shard_map/ppermute | solution.py:14
  74.4 9.1 %collective-permute-start.14 = (f32[2,1,32,128]{3,2,1,0:T(8,128)S(1)}, f32[2,1,32,128]{3,2,1,0:T(8,128)S(1)}, u32[]{:S(2)}, u32[]{:S(2)}) collective-permute-start(f32[2,1,32,128]{3,2,1,0:T(8,128)S(1)} %pad_maximum_fusion.11), channel_id=1, source_target_pairs={{0,8},{8,16},{16,24},{24,32},{32,40},{40,48},{48,56},{56,64},{64,7... | collective-permute-start | bytes 98312 | tf_op jit(solution)/shard_map/ppermute | solution.py:14
  76.4 9.4 %collective-permute-start.15 = (f32[1,8,1,128]{3,1,2,0:T(8,128)S(1)}, f32[1,8,1,128]{3,1,2,0:T(8,128)S(1)}, u32[]{:S(2)}, u32[]{:S(2)}) collective-permute-start(f32[1,8,1,128]{3,1,2,0:T(8,128)S(1)} %bitcast.476), channel_id=1, source_target_pairs={{1,0},{2,1},{3,2},{4,3},{5,4},{6,5},{7,6},{9,8},{10,9},{11,10},{12... | collective-permute-start | bytes 12296 | tf_op jit(solution)/shard_map/ppermute | solution.py:14
  77.8 8.1 %collective-permute-start.10 = (f32[1,1,32,128]{3,2,1,0:T(8,128)S(1)}, f32[1,1,32,128]{3,2,1,0:T(8,128)S(1)}, u32[]{:S(2)}, u32[]{:S(2)}) collective-permute-start(f32[1,1,32,128]{3,2,1,0:T(8,128)S(1)} %slice_bitcast_fusion.22), channel_id=1, source_target_pairs={{8,0},{16,8},{24,16},{32,24},{40,32},{48,40},{56,48},{64,56},{72,6... | collective-permute-start | bytes 49160 | tf_op jit(solution)/shard_map/ppermute | solution.py:14
  89.0 23.3 %all-to-all-start = ((f32[2,3,1,72,256]{4,0,2,1,3:T(2,128)}), f32[2,3,1,72,256]{4,0,2,1,3:T(2,128)S(1)}, u32[]{:S(2)}, u32[]{:S(2)}) async-start(f32[2,3,1,72,256]{4,0,2,1,3:T(2,128)} %pad_maximum_fusion.2), calls=%async_computation | async-start | bytes 884736 | tf_op jit(solution)/shard_map/all_to_all | solution.py:159
  128.2 29.9 %all-to-all-start.1 = ((f32[2,3,1,256,72]{4,2,1,0,3:T(1,128)}), f32[2,3,1,256,72]{4,2,1,0,3:T(1,128)S(1)}, u32[]{:S(2)}, u32[]{:S(2)}) async-start(f32[2,3,1,256,72]{4,2,1,0,3:T(1,128)} %copy.164), calls=%async_computation.1 | async-start | bytes 1572864 | tf_op jit(solution)/shard_map/all_to_all | solution.py:167
  225.6 22.8 %all-to-all-start.2 = ((f32[64,1,1728]{2,1,0:T(1,128)}), f32[64,1,1728]{2,1,0:T(1,128)S(1)}, u32[]{:S(2)}, u32[]{:S(2)}) async-start(f32[64,1,1728]{2,1,0:T(1,128)} %reshape.528), calls=%async_computation.2 | async-start | bytes 917504 | tf_op jit(solution)/shard_map/all_to_all | solution.py:211
  288.0 29.9 %all-to-all-start.3 = ((f32[8,2,3,1,32,72]{5,4,3,2,1,0:T(8,128)}), f32[8,2,3,1,32,72]{5,4,3,2,1,0:T(8,128)S(1)}, u32[]{:S(2)}, u32[]{:S(2)}) async-start(f32[8,2,3,1,32,72]{5,4,3,2,1,0:T(8,128)} %constant_dynamic-update-slice_fusion), calls=%async_computation.3 | async-start | bytes 1572864 | tf_op jit(solution)/shard_map/all_to_all | solution.py:220
  (5 other events, 29.1 us)
